TPU v7x, 32 devices: a whole 2x2x4 slice. The times are simulated.
32 devices in a mesh: row: 4 (over y, x), col: 8 (over z, core).
Axes of the slice: x: 2, y: 2, z: 4, core: 2. Of those that a mesh axis runs over, the one named last changes fastest.
Arguments:
- features: bfloat16 [16384, 256], P(('col', 'row')), may hold values from -6 to 6
- weight: bfloat16 [256, 256], replicated, may hold values from -0.375 to 0.375
- cotangent: bfloat16 [16384, 256], P(('row', 'col')), may hold values from -6 to 6
- block_index: int32 [4, 8, 32], P('row', 'col'), may hold values from 0 to 511, as said below
- block_count: int32 [4, 8], P('row', 'col'), may hold values from 1 to 32, as said below
- block_values: bfloat16 [4, 8, 32, 128, 128], P('row', 'col'), may hold values from -0.25 to 0.25
Outputs:
- hidden_out: bfloat16 [16384, 256], P(('row', 'col'))
- input_grad: bfloat16 [16384, 256], P(('col', 'row'))
- weight_grad: float32 [256, 256], replicated
Inputs may be any that keep to these rules, and one draw needn't show every extreme that they name: `block_index`: the 32 entries of one tile are distinct; slots at or after the tile's count hold blocks that are not used. `block_count`: at least one tile holds exactly 32 blocks.
All inputs are finite; a program needn't handle non-finite values.
Results may differ from a plain program's by a relative error of at most 0.015.
Values may be sent and summed in bfloat16 or wider, within the bound.
No kernel may reach another device: no remote copies, remote signals or barrier semaphores. Data moves between devices by JAX's collectives and lax.ppermute only.
A program may use at most 64 MiB of HBM per device.

v0:
```python
import math
import jax
import jax.numpy as jnp
from jax import lax
from jax.sharding import PartitionSpec as P

GROUP = 32


def forward_tile(blocks_in, values, index, count, rows_out):
    ncols = blocks_in.shape[0]
    size = blocks_in.shape[1]
    width = blocks_in.shape[2]
    lanes = jnp.arange(GROUP, dtype=jnp.int32)
    targets = jnp.arange(rows_out, dtype=jnp.int32)

    def forward_advance(group_id, totals):
        start = (group_id * GROUP).astype(jnp.int32)
        live = start + lanes < count
        picked = jnp.take(blocks_in, index % ncols, axis=0)
        product = jnp.einsum("gij,gjd->gid", values, picked, preferred_element_type=jnp.float32)
        selector = ((index // ncols)[None, :] == targets[:, None]) & live[None, :]
        return totals + jnp.einsum(
            "rg,gid->rid", selector.astype(jnp.float32), product, precision=lax.Precision.HIGHEST
        )

    zeros = jnp.zeros((rows_out, size, width), jnp.float32)
    groups = (count + GROUP - 1) // GROUP
    return lax.fori_loop(jnp.int32(0), groups, forward_advance, zeros)


def backward_tile(blocks_grad, values, index, count, cols_out):
    size = blocks_grad.shape[1]
    width = blocks_grad.shape[2]
    lanes = jnp.arange(GROUP, dtype=jnp.int32)
    targets = jnp.arange(cols_out, dtype=jnp.int32)

    def backward_advance(group_id, totals):
        start = (group_id * GROUP).astype(jnp.int32)
        live = start + lanes < count
        picked = jnp.take(blocks_grad, index // cols_out, axis=0)
        product = jnp.einsum("gij,gid->gjd", values, picked, preferred_element_type=jnp.float32)
        selector = ((index % cols_out)[None, :] == targets[:, None]) & live[None, :]
        return totals + jnp.einsum(
            "cg,gjd->cjd", selector.astype(jnp.float32), product, precision=lax.Precision.HIGHEST
        )

    zeros = jnp.zeros((cols_out, size, width), jnp.float32)
    groups = (count + GROUP - 1) // GROUP
    return lax.fori_loop(jnp.int32(0), groups, backward_advance, zeros)


def body(features, weight, cotangent, block_index, block_count, block_values):
    row_total = lax.axis_size("row")
    col_total = lax.axis_size("col")
    rows = features.shape[0]
    width = features.shape[1]
    size = block_values.shape[-1]
    block_rows = rows * col_total // size
    block_cols = rows * row_total // size
    index = block_index[0, 0]
    count = block_count[0, 0]
    values = block_values[0, 0]
    gathered = lax.all_gather(features, "row", axis=0, tiled=True)
    projected = jnp.dot(gathered, weight, preferred_element_type=jnp.float32).astype(jnp.bfloat16)
    partial_out = forward_tile(
        projected.reshape(block_cols, size, width), values, index, count, block_rows
    )
    summed_out = lax.psum_scatter(
        partial_out.reshape(block_rows * size, width).astype(jnp.bfloat16),
        "col",
        scatter_dimension=0,
        tiled=True,
    )
    grad_rows = lax.all_gather(cotangent, "col", axis=0, tiled=True)
    partial_back = backward_tile(
        grad_rows.reshape(block_rows, size, width), values, index, count, block_cols
    )
    partial_back = partial_back.reshape(block_cols * size, width)
    grad_sum = lax.psum_scatter(
        partial_back.astype(jnp.bfloat16), "row", scatter_dimension=0, tiled=True
    ).astype(jnp.float32)
    input_grad = jnp.dot(
        grad_sum, weight.astype(jnp.float32).T, precision=lax.Precision.HIGHEST
    ).astype(jnp.bfloat16)
    term = jnp.einsum(
        "nd,ne->de", gathered, partial_back.astype(jnp.bfloat16), preferred_element_type=jnp.float32
    )
    total = lax.psum(term, ("row", "col"))
    nodes = rows * row_total * col_total
    weight_grad = total / math.sqrt(nodes)
    return (summed_out, input_grad, weight_grad)


def solution(mesh):
    in_specs = (
        P(("col", "row"), None),
        P(),
        P(("row", "col"), None),
        P("row", "col", None),
        P("row", "col"),
        P("row", "col", None, None, None),
    )
    out_specs = (P(("row", "col"), None), P(("col", "row"), None), P())
    return jax.shard_map(body, mesh=mesh, in_specs=in_specs, out_specs=out_specs, check_vma=False)
```

profile of v0, /device:TPU:0, one launch (start us, length us, event | category | flops | bytes accessed | tf_op | source)
XLA Modules:
  0.0 277.0 jit_solution(4447913578105518089)
XLA Ops:
  8.0 0.7 all-gather.3.cloned.1.call-update
  11.4 30.1 %all-gather.5.cloned.1.call-done = bf16[4096,256]{1,0:T(8,128)(2,1)} async-done(((bf16[512,256]{1,0:T(8,128)(2,1)}), bf16[4096,256]{1,0:T(8,128)(2,1)}) %all-gather.5.cloned.1.call-update) | async-done | bytes 2097168 | tf_op jit(solution)/shard_map/all_gather | solution.py:75
  41.5 3.6 %gather_fusion.1 = bf16[32,128,256]{2,1,0:T(8,128)(2,1)} fusion(bf16[32,128,256]{2,1,0:T(8,128)(2,1)} %bitcast.94, s32[1024]{0:T(1024)S(1)} %pad_clamp_fusion.1), kind=kCustom, calls=%fused_computation.1 | custom fusion | bytes 4194432 | tf_op jit(solution)/shard_map/while/body/jit(_take)/gather | solution.py:41
  45.8 15.6 %while.34 = (s32[]{:T(128)}, f32[16,128,256]{2,0,1:T(8,128)S(1)}, s32[]{:T(128)}, s32[32]{0:T(128)S(1)}, s32[32]{0:T(128)S(1)}, /*index=5*/s32[]{:T(128)}, s32[3...) while((s32[]{:T(128)}, f32[16,128,256]{2,0,1:T(8,128)S(1)}, ...), condition=%wide.region_4.5_spmd.clone, body=%wide.region_3.4_spmd.clone.sunk | while | flops 471336928 | bytes 24118400 | solution.py:50
  46.5 4.6 %fusion.69 = f32[32,256,128]{2,1,0:T(8,128)} fusion(bf16[32,128,128]{2,1,0:T(8,128)(2,1)} %get-tuple-element.889, bf16[32,128,256]{2,1,0:T(8,128)(2,1)} %get-tuple-element.888, pred[32]{0:T(512)(128)(4,1)S(1)} %get-tuple-element.805), kind=kOutput, calls=%fused_computation.7.clone.1 | convolution fusion | flops 269484032 | bytes 7340064 | tf_op jit(solution)/shard_map/while/body/gij,gid->gjd/dot_general | solution.py:42
  51.1 5.5 %copy.20 = f32[32,256,128]{1,0,2:T(8,128)} copy(f32[32,256,128]{2,1,0:T(8,128)} %fusion.69) | data formatting | bytes 8388608 | tf_op jit(solution)/shard_map/while/body/gij,gid->gjd/dot_general | solution.py:42
  56.6 4.8 %fusion.70 = f32[16,128,256]{2,0,1:T(8,128)S(1)} fusion(f32[16,128,256]{2,0,1:T(8,128)S(1)} %get-tuple-element.871, f32[32,256,128]{1,0,2:T(8,128)} %copy.20, s32[32]{0:T(128)S(1)} %and_select_fusion.6, pred[32]{0:T(512)(128)(4,1)S(1)} %get-tuple-element.806), kind=kOutput, calls=%fused_computation.10.clone.1 | convolution fusion | flops 201851904 | bytes 8388768 | tf_op jit(solution)/shard_map/while/body/cg,gjd->cjd/dot_general | solution.py:44
  61.4 1.1 copy.17
  62.6 6.7 %all-gather.3.cloned.1.call-done = bf16[2048,256]{1,0:T(8,128)(2,1)} async-done(((bf16[512,256]{1,0:T(8,128)(2,1)}), bf16[2048,256]{1,0:T(8,128)(2,1)}) %all-gather.3.cloned.1.call-update) | async-done | bytes 1048592 | tf_op jit(solution)/shard_map/all_gather | solution.py:64
  69.3 2.5 convolution_bitcast_fusion
  72.4 2.5 broadcast_in_dim.62
  74.9 18.6 %while.35 = (s32[]{:T(128)}, f32[32,128,256]{2,0,1:T(8,128)}, s32[]{:T(128)}, s32[1,32]{1,0:T(1,128)S(1)}, s32[32]{0:T(128)S(1)}, /*index=5*/s32[1,32]{1,0:T(1,1...) while((s32[]{:T(128)}, f32[32,128,256]{2,0,1:T(8,128)}, ...), condition=%wide.region_1.2_spmd.clone.clone, body=%wide.region_0.1_spmd.clone.clone.sunk | while | flops 673190272 | bytes 32511760 | solution.py:29
  75.6 0.7 gather_fusion
  76.3 4.0 %fusion.76 = f32[32,256,128]{2,1,0:T(8,128)} fusion(bf16[32,128,128]{2,1,0:T(8,128)(2,1)} %get-tuple-element.856, bf16[32,128,256]{2,1,0:T(8,128)(2,1)S(1)} %gather_fusion, pred[32]{0:T(512)(128)(4,1)S(1)} %get-tuple-element.818), kind=kOutput, calls=%fused_computation.30.clone.1 | convolution fusion | flops 269484032 | bytes 7340064 | tf_op jit(solution)/shard_map/while/body/gij,gjd->gid/dot_general | solution.py:21
  80.3 5.5 %copy.21 = f32[32,256,128]{1,0,2:T(8,128)} copy(f32[32,256,128]{2,1,0:T(8,128)} %fusion.76) | data formatting | bytes 8388608 | tf_op jit(solution)/shard_map/while/body/gij,gjd->gid/dot_general | solution.py:21
  85.8 7.7 %fusion.78 = f32[32,128,256]{2,0,1:T(8,128)} fusion(f32[32,128,256]{2,0,1:T(8,128)} %get-tuple-element.834, f32[32,256,128]{1,0,2:T(8,128)} %copy.21, s32[32]{0:T(128)S(1)} %fusion.77, pred[32]{0:T(512)(128)(4,1)S(1)} %get-tuple-element.819), kind=kOutput, calls=%fused_computation.29.clone.1 | convolution fusion | flops 403703808 | bytes 12583072 | tf_op jit(solution)/shard_map/while/body/rg,gid->rid/dot_general | solution.py:23
  93.5 2.5 convert_element_type.25
  96.0 2.5 copy.11
  98.6 103.3 %all-reduce.2.cloned.1.call-done = f32[256,256]{0,1:T(8,128)} async-done(((f32[256,256]{0,1:T(8,128)}), f32[256,256]{0,1:T(8,128)}) %all-reduce.2.cloned.1.call-update) | async-done | bytes 262160 | tf_op jit(solution)/shard_map/psum | solution.py:89
  201.9 1.0 broadcast_multiply_fusion
  202.9 0.8 copy.13
  203.7 27.9 %reduce-scatter.5.cloned.1.call-done = bf16[512,256]{1,0:T(8,128)(2,1)} async-done(((bf16[2048,256]{1,0:T(8,128)(2,1)}), bf16[512,256]{1,0:T(8,128)(2,1)}) %reduce-scatter.5.cloned.1.call-update) | async-done | bytes 262160 | tf_op jit(solution)/shard_map/reduce_scatter | solution.py:80
  231.7 1.9 convolution_convert_fusion.1
  233.6 36.9 %reduce-scatter.3.cloned.1.call-done = bf16[512,256]{1,0:T(8,128)(2,1)} async-done(((bf16[4096,256]{1,0:T(8,128)(2,1)}), bf16[512,256]{1,0:T(8,128)(2,1)}) %reduce-scatter.3.cloned.1.call-update) | async-done | bytes 262160 | tf_op jit(solution)/shard_map/reduce_scatter | solution.py:69
  (29 shorter events, 5.4 us)
Async XLA Ops:
  7.2 64.7 %copy-start = (bf16[256,256]{1,0:T(8,128)(2,1)S(1)}, bf16[256,256]{1,0:T(8,128)(2,1)}, u32[]{:S(2)}) copy-start(bf16[256,256]{1,0:T(8,128)(2,1)} %param.11) | copy-start | bytes 393220
  7.2 34.3 %all-gather.5.cloned.1.call-start = ((), (), s32[]{:S(2)}) async-start(), calls=%async_computation.4 | async-start | bytes 2359296 | tf_op jit(solution)/shard_map/all_gather | solution.py:75
  7.9 61.3 %all-gather.3.cloned.1.call-start = ((), (), s32[]{:S(2)}) async-start(), calls=%async_computation.2 | async-start | bytes 1310720 | tf_op jit(solution)/shard_map/all_gather | solution.py:64
  8.7 193.3 %all-reduce.2.cloned.1.call-start = ((), (), s32[]{:S(2)}) async-start(), calls=%async_computation.6 | async-start | bytes 524288 | tf_op jit(solution)/shard_map/psum | solution.py:89
  45.1 0.7 copy-start.3
  62.6 9.2 %copy-start.1 = (bf16[16,128,256]{2,1,0:T(8,128)(2,1)}, bf16[16,128,256]{2,1,0:T(8,128)(2,1)S(1)}, u32[]{:S(2)}) copy-start(bf16[16,128,256]{2,1,0:T(8,128)(2,1)S(1)} %copy.17) | copy-start | bytes 3145732
  69.3 2.6 copy-start.2
  71.8 159.9 %reduce-scatter.5.cloned.1.call-start = ((), (), s32[]{:S(2)}) async-start(), calls=%async_computation.5 | async-start | bytes 1310720 | tf_op jit(solution)/shard_map/reduce_scatter | solution.py:80
  72.4 198.1 %reduce-scatter.3.cloned.1.call-start = ((), (), s32[]{:S(2)}) async-start(), calls=%async_computation.3 | async-start | bytes 2359296 | tf_op jit(solution)/shard_map/reduce_scatter | solution.py:69
Sparse Core Ops, SparseCore 0:
  9.6 31.8 all-gather.4
  43.3 25.8 all-gather.2
  75.3 126.5 all-reduce.1
  204.7 26.9 reduce-scatter.4
  234.4 36.0 reduce-scatter.2
where the time goes:
time: 278 us; the launch traced here: 277 us
  waiting for transfers between devices  206 us (74%)
  matrix products  26 us (9%)
  local copies, waits for them, and re-layouts  22.9 us (8%)
  between operations  14.5 us (5%)
  other arithmetic  6.83 us (2%)
    psum x1, waiting for transfers between devices, body(): total = lax.psum(term, ('row', 'col'))  103 us
    reduce_scatter x1, waiting for transfers between devices, body(): lax.psum_scatter(partial_out.reshape(block_rows * size, width).astype(jnp...  36.9 us
    all_gather x1, waiting for transfers between devices, body(): grad_rows = lax.all_gather(cotangent, 'col', axis=0, tiled=True)  30.1 us
    reduce_scatter x1, waiting for transfers between devices, body(): lax.psum_scatter(partial_back.astype(jnp.bfloat16), 'row', scatter_dimens...  27.9 us
    dot_general x1, matrix products, forward_advance(): jnp.einsum('rg,gid->rid', selector.astype(jnp.float32), product, precisio...  7.68 us
    all_gather x1, waiting for transfers between devices, body(): gathered = lax.all_gather(features, 'row', axis=0, tiled=True)  6.68 us
  transfers between devices with their start and end apart: 5, of which 5 were waited for; matrix products, arithmetic and copies ran while one was open for 19% of the time, Pallas kernels for 0%

commit v1 on v0

--- a/solution.py
+++ b/solution.py
@@ -5,6 +5,27 @@
 from jax.sharding import PartitionSpec as P
 
 GROUP = 32
+
+
+def divide_cube(base_x, dim_no):
+    res = list(base_x.shape[1:])
+    res[dim_no] *= base_x.shape[0]
+    return jnp.moveaxis(base_x, 0, dim_no).reshape(res)
+
+
+def cells_get(content, named_axis):
+    block_last, response = (jax.lax.axis_size(named_axis), jax.lax.axis_index(named_axis))
+    q_next, newest = (content[None], 1)
+    while newest < block_last:
+        plain = jax.lax.ppermute(q_next, named_axis, [(k, k ^ newest) for k in range(block_last)])
+        y2 = response & newest == 0
+        q_next = jnp.concatenate([jnp.where(y2, q_next, plain), jnp.where(y2, plain, q_next)])
+        newest *= 2
+    return q_next
+
+
+def replace_the_packet(z_in, buf, row_dim):
+    return divide_cube(cells_get(z_in, buf), row_dim)
 
 
 def forward_tile(blocks_in, values, index, count, rows_out):
@@ -72,7 +93,7 @@
         scatter_dimension=0,
         tiled=True,
     )
-    grad_rows = lax.all_gather(cotangent, "col", axis=0, tiled=True)
+    grad_rows = replace_the_packet(cotangent, "col", 0)
     partial_back = backward_tile(
         grad_rows.reshape(block_rows, size, width), values, index, count, block_cols
     )

time: 278 us -> 299 us (1.076)
  waiting for transfers between devices: 206 us -> 224 us
  starting transfers between devices: 0.2 us -> 6.54 us
    ppermute x0 -> x3, waiting for transfers between devices: none -> 58 us  [cells_get(): jax.lax.ppermute(q_next, named_axis, [(k, k ^ newest) for k in range(bloc...]
    all_gather x1 -> x0, waiting for transfers between devices: 30.1 us -> none  [body(): grad_rows = lax.all_gather(cotangent, 'col', axis=0, tiled=True)]
    all_gather x1, waiting for transfers between devices: 6.68 us -> 0.02 us  [body(): gathered = lax.all_gather(features, 'row', axis=0, tiled=True)]
    ppermute x0 -> x3, starting transfers between devices: none -> 6.37 us  [cells_get(): jax.lax.ppermute(q_next, named_axis, [(k, k ^ newest) for k in range(bloc...]
  transfers between devices with their start and end apart: 5 -> 7, of which waited for: 5 -> 6; matrix products, arithmetic and copies ran while one was open for 19% -> 17% of each run, Pallas kernels for 0% -> 0%
where the time goes in v1:
time: 299 us
  waiting for transfers between devices  224 us (75%)
  matrix products  26.3 us (9%)
  local copies, waits for them, and re-layouts  21 us (7%)
  between operations  14.6 us (5%)
  starting transfers between devices  6.54 us (2%)
  other arithmetic  6.4 us (2%)
    psum x1, waiting for transfers between devices, body(): total = lax.psum(term, ('row', 'col'))  101 us
    ppermute x3, waiting for transfers between devices, cells_get(): jax.lax.ppermute(q_next, named_axis, [(k, k ^ newest) for k in range(bloc...  58 us
    reduce_scatter x1, waiting for transfers between devices, body(): lax.psum_scatter(partial_out.reshape(block_rows * size, width).astype(jnp...  36.6 us
    reduce_scatter x1, waiting for transfers between devices, body(): lax.psum_scatter(partial_back.astype(jnp.bfloat16), 'row', scatter_dimens...  28.1 us
    dot_general x1, matrix products, forward_advance(): jnp.einsum('rg,gid->rid', selector.astype(jnp.float32), product, precisio...  7.69 us
    ppermute x3, starting transfers between devices, cells_get(): jax.lax.ppermute(q_next, named_axis, [(k, k ^ newest) for k in range(bloc...  6.37 us
  transfers between devices with their start and end apart: 7, of which 6 were waited for; matrix products, arithmetic and copies ran while one was open for 17% of the time, Pallas kernels for 0%

profile of v1, /device:TPU:0, one launch (start us, length us, event | category | flops | bytes accessed | tf_op | source)
XLA Modules:
  0.0 298.7 jit_solution(5794929942287257078)
XLA Ops:
  7.8 1.4 collective-permute-done
  9.2 1.0 broadcast_select_fusion.5
  10.2 3.0 %collective-permute-start.1 = (bf16[2,512,256]{2,1,0:T(8,128)(2,1)S(1)}, bf16[2,512,256]{2,1,0:T(8,128)(2,1)S(1)}, u32[]{:S(2)}, u32[]{:S(2)}) collective-permute-start(bf16[2,512,256]{2,1,0:T(8,128)(2,1)S(1)} %pad_maximum_fusion.2), channel_id=1, source_target_pairs={{0,2},{1,3},{2,0},{3,1},{4,6},{5,7},{6,4},{7,5},{8,10},{9,11},{10,... | collective-permute-start | bytes 1572872 | tf_op jit(solution)/shard_map/ppermute | solution.py:20
  13.2 12.2 %collective-permute-done.1 = bf16[2,512,256]{2,1,0:T(8,128)(2,1)S(1)} collective-permute-done((bf16[2,512,256]{2,1,0:T(8,128)(2,1)S(1)}, bf16[2,512,256]{2,1,0:T(8,128)(2,1)S(1)}, u32[]{:S(2)}, u32[]{:S(2)}) %collective-permute-start.1) | collective-permute-done | bytes 524320 | tf_op jit(solution)/shard_map/ppermute | solution.py:20
  25.6 2.8 collective-permute-start.2
  29.2 44.4 %collective-permute-done.2 = bf16[4,512,256]{2,1,0:T(8,128)(2,1)S(1)} collective-permute-done((bf16[4,512,256]{2,1,0:T(8,128)(2,1)S(1)}, bf16[4,512,256]{2,1,0:T(8,128)(2,1)S(1)}, u32[]{:S(2)}, u32[]{:S(2)}) %collective-permute-start.2) | collective-permute-done | bytes 1048608 | tf_op jit(solution)/shard_map/ppermute | solution.py:20
  74.0 2.1 gather_fusion.1
  76.3 15.7 %while.34 = (s32[]{:T(128)}, f32[16,128,256]{2,0,1:T(8,128)S(1)}, s32[]{:T(128)}, s32[32]{0:T(128)S(1)}, s32[32]{0:T(128)S(1)}, /*index=5*/s32[]{:T(128)}, s32[3...) while((s32[]{:T(128)}, f32[16,128,256]{2,0,1:T(8,128)S(1)}, ...), condition=%wide.region_4.5_spmd.clone, body=%wide.region_3.4_spmd.clone.sunk | while | flops 471336928 | bytes 24118400 | solution.py:71
  77.0 4.6 %fusion.69 = f32[32,256,128]{2,1,0:T(8,128)} fusion(bf16[32,128,128]{2,1,0:T(8,128)(2,1)} %get-tuple-element.895, bf16[32,128,256]{2,1,0:T(8,128)(2,1)} %get-tuple-element.894, pred[32]{0:T(512)(128)(4,1)S(1)} %get-tuple-element.811), kind=kOutput, calls=%fused_computation.7.clone.1 | convolution fusion | flops 269484032 | bytes 7340064 | tf_op jit(solution)/shard_map/while/body/gij,gid->gjd/dot_general | solution.py:63
  81.6 5.5 %copy.20 = f32[32,256,128]{1,0,2:T(8,128)} copy(f32[32,256,128]{2,1,0:T(8,128)} %fusion.69) | data formatting | bytes 8388608 | tf_op jit(solution)/shard_map/while/body/gij,gid->gjd/dot_general | solution.py:63
  87.2 4.8 %fusion.70 = f32[16,128,256]{2,0,1:T(8,128)S(1)} fusion(f32[16,128,256]{2,0,1:T(8,128)S(1)} %get-tuple-element.877, f32[32,256,128]{1,0,2:T(8,128)} %copy.20, s32[32]{0:T(128)S(1)} %and_select_fusion.6, pred[32]{0:T(512)(128)(4,1)S(1)} %get-tuple-element.812), kind=kOutput, calls=%fused_computation.10.clone.1 | convolution fusion | flops 201851904 | bytes 8388768 | tf_op jit(solution)/shard_map/while/body/cg,gjd->cjd/dot_general | solution.py:65
  92.0 1.1 copy.17
  93.2 2.8 convolution_bitcast_fusion
  96.8 2.5 broadcast_in_dim.65
  99.3 18.6 %while.35 = (s32[]{:T(128)}, f32[32,128,256]{2,0,1:T(8,128)}, s32[]{:T(128)}, s32[1,32]{1,0:T(1,128)S(1)}, s32[32]{0:T(128)S(1)}, /*index=5*/s32[1,32]{1,0:T(1,1...) while((s32[]{:T(128)}, f32[32,128,256]{2,0,1:T(8,128)}, ...), condition=%wide.region_1.2_spmd.clone.clone, body=%wide.region_0.1_spmd.clone.clone.sunk | while | flops 673190272 | bytes 32511760 | solution.py:50
  100.7 4.0 %fusion.76 = f32[32,256,128]{2,1,0:T(8,128)} fusion(bf16[32,128,128]{2,1,0:T(8,128)(2,1)} %get-tuple-element.862, bf16[32,128,256]{2,1,0:T(8,128)(2,1)S(1)} %gather_fusion, pred[32]{0:T(512)(128)(4,1)S(1)} %get-tuple-element.824), kind=kOutput, calls=%fused_computation.30.clone.1 | convolution fusion | flops 269484032 | bytes 7340064 | tf_op jit(solution)/shard_map/while/body/gij,gjd->gid/dot_general | solution.py:42
  104.7 5.5 %copy.21 = f32[32,256,128]{1,0,2:T(8,128)} copy(f32[32,256,128]{2,1,0:T(8,128)} %fusion.76) | data formatting | bytes 8388608 | tf_op jit(solution)/shard_map/while/body/gij,gjd->gid/dot_general | solution.py:42
  110.2 7.7 %fusion.78 = f32[32,128,256]{2,0,1:T(8,128)} fusion(f32[32,128,256]{2,0,1:T(8,128)} %get-tuple-element.840, f32[32,256,128]{1,0,2:T(8,128)} %copy.21, s32[32]{0:T(128)S(1)} %fusion.77, pred[32]{0:T(512)(128)(4,1)S(1)} %get-tuple-element.825), kind=kOutput, calls=%fused_computation.29.clone.1 | convolution fusion | flops 403703808 | bytes 12583072 | tf_op jit(solution)/shard_map/while/body/rg,gid->rid/dot_general | solution.py:44
  117.9 2.5 convert_element_type.25
  120.4 2.5 copy.11
  123.0 100.7 %all-reduce.2.cloned.1.call-done = f32[256,256]{0,1:T(8,128)} async-done(((f32[256,256]{0,1:T(8,128)}), f32[256,256]{0,1:T(8,128)}) %all-reduce.2.cloned.1.call-update) | async-done | bytes 262160 | tf_op jit(solution)/shard_map/psum | solution.py:110
  225.5 28.1 %reduce-scatter.5.cloned.1.call-done = bf16[512,256]{1,0:T(8,128)(2,1)} async-done(((bf16[2048,256]{1,0:T(8,128)(2,1)}), bf16[512,256]{1,0:T(8,128)(2,1)}) %reduce-scatter.5.cloned.1.call-update) | async-done | bytes 262160 | tf_op jit(solution)/shard_map/reduce_scatter | solution.py:101
  253.6 1.9 convolution_convert_fusion.1
  255.5 36.6 %reduce-scatter.3.cloned.1.call-done = bf16[512,256]{1,0:T(8,128)(2,1)} async-done(((bf16[4096,256]{1,0:T(8,128)(2,1)}), bf16[512,256]{1,0:T(8,128)(2,1)}) %reduce-scatter.3.cloned.1.call-update) | async-done | bytes 262160 | tf_op jit(solution)/shard_map/reduce_scatter | solution.py:90
  (38 shorter events, 6.1 us)
Async XLA Ops:
  7.2 88.9 %copy-start = (bf16[256,256]{1,0:T(8,128)(2,1)S(1)}, bf16[256,256]{1,0:T(8,128)(2,1)}, u32[]{:S(2)}) copy-start(bf16[256,256]{1,0:T(8,128)(2,1)} %param.11) | copy-start | bytes 393220
  7.2 86.0 %all-gather.2.cloned.1.call-start = ((), (), s32[]{:S(2)}) async-start(), calls=%async_computation.2 | async-start | bytes 1310720 | tf_op jit(solution)/shard_map/all_gather | solution.py:85
  7.2 1.9 collective-permute-start
  10.2 15.2 %collective-permute-start.1 = (bf16[2,512,256]{2,1,0:T(8,128)(2,1)S(1)}, bf16[2,512,256]{2,1,0:T(8,128)(2,1)S(1)}, u32[]{:S(2)}, u32[]{:S(2)}) collective-permute-start(bf16[2,512,256]{2,1,0:T(8,128)(2,1)S(1)} %pad_maximum_fusion.2), channel_id=1, source_target_pairs={{0,2},{1,3},{2,0},{3,1},{4,6},{5,7},{6,4},{7,5},{8,10},{9,11},{10,... | collective-permute-start | bytes 1572872 | tf_op jit(solution)/shard_map/ppermute | solution.py:20
  13.2 16.0 %copy-start.3 = (s32[1,1,32]{2,1,0:T(1,128)S(1)}, s32[1,1,32]{2,1,0:T(1,128)}, u32[]{:S(2)}) copy-start(s32[1,1,32]{2,1,0:T(1,128)} %param.13) | copy-start | bytes 388
  25.6 48.1 %collective-permute-start.2 = (bf16[4,512,256]{2,1,0:T(8,128)(2,1)S(1)}, bf16[4,512,256]{2,1,0:T(8,128)(2,1)S(1)}, u32[]{:S(2)}, u32[]{:S(2)}) collective-permute-start(bf16[4,512,256]{2,1,0:T(8,128)(2,1)S(1)} %pad_maximum_fusion.1), channel_id=1, source_target_pairs={{0,4},{1,5},{2,6},{3,7},{4,0},{5,1},{6,2},{7,3},{8,12},{9,13},{10,... | collective-permute-start | bytes 3145736 | tf_op jit(solution)/shard_map/ppermute | solution.py:20
  28.5 195.2 %all-reduce.2.cloned.1.call-start = ((), (), s32[]{:S(2)}) async-start(), calls=%async_computation.5 | async-start | bytes 524288 | tf_op jit(solution)/shard_map/psum | solution.py:110
  93.1 2.9 copy-start.1
  93.2 2.9 copy-start.2
  96.0 157.6 %reduce-scatter.5.cloned.1.call-start = ((), (), s32[]{:S(2)}) async-start(), calls=%async_computation.4 | async-start | bytes 1310720 | tf_op jit(solution)/shard_map/reduce_scatter | solution.py:101
  96.7 195.4 %reduce-scatter.3.cloned.1.call-start = ((), (), s32[]{:S(2)}) async-start(), calls=%async_computation.3 | async-start | bytes 2359296 | tf_op jit(solution)/shard_map/reduce_scatter | solution.py:90
Sparse Core Ops, SparseCore 0:
  28.6 25.7 all-gather.1
  96.1 127.5 all-reduce.1
  226.6 26.9 reduce-scatter.4
  256.3 35.7 reduce-scatter.2
